TPU v7x, 512 devices: a whole 4x8x8 slice. The times are simulated.
512 devices in a mesh: ctx: 64 (over x, z, core), head: 8 (over y).
Axes of the slice: x: 4, y: 8, z: 8, core: 2. Of those that a mesh axis runs over, the one named last changes fastest.
Arguments:
- queries: bfloat16 [12288, 4096], P('ctx', 'head'), may hold values from -6 to 6
- key_rows: bfloat16 [12288, 4096], P('ctx', 'head'), may hold values from -6 to 6
- value_rows: bfloat16 [12288, 4096], P('ctx', 'head'), may hold values from -120 to 120
- gate_rows: bfloat16 [12288, 4096], P('ctx', 'head'), may hold values from -8 to 8
- cotangent: bfloat16 [12288, 4096], P('ctx', 'head'), may hold values from -6 to 6
Outputs:
- grad_queries: bfloat16 [12288, 4096], P('ctx', 'head')
- grad_keys: bfloat16 [12288, 4096], P('ctx', 'head')
- grad_values: bfloat16 [12288, 4096], P('ctx', 'head')
- grad_gates: bfloat16 [12288, 4096], P('ctx', 'head')
All inputs are finite; a program needn't handle non-finite values.
Results may differ from a plain program's by a relative error of at most 0.0065.
Values sent between devices are 32-bit elements; how exact they have to be, the bound alone decides.
A program may use at most 64 MiB of HBM per device.

v0:
```python
import jax
import jax.numpy as jnp
from jax import lax
from jax.sharding import PartitionSpec as P

H = 32
DH = 128


EPSILON = 1e-06


def carried_in(part, axis, combine, identity, reverse):
    count = lax.axis_size(axis)
    place = lax.axis_index(axis)
    ahead = count - 1 - place if reverse else place
    gathered = lax.all_gather(part, axis)
    state = jnp.zeros_like(part) + jnp.asarray(identity, part.dtype)

    def one(step, state):
        source = count - 1 - step if reverse else step
        return combine(state, lax.dynamic_index_in_dim(gathered, source, 0, False))

    return lax.fori_loop(0, ahead, one, state)


def silu_slope(x):
    sig = jax.nn.sigmoid(x)
    return sig * (1.0 + x * (1.0 - sig))


def add_states(earlier, later):
    return earlier + later


def per_device(queries, key_rows, value_rows, gate_rows, cotangent):
    rows, width = queries.shape
    heads = width // DH
    full_width = H * DH
    q_float = queries.astype(jnp.float32)
    k_float = key_rows.astype(jnp.float32)
    lifted_q = jax.nn.silu(q_float).astype(jnp.bfloat16).reshape(rows, heads, DH)
    lifted_k = jax.nn.silu(k_float).astype(jnp.bfloat16).reshape(rows, heads, DH)
    values = value_rows.reshape(rows, heads, DH)
    causal = lax.broadcasted_iota(jnp.int32, (rows, rows), 0) >= lax.broadcasted_iota(
        jnp.int32, (rows, rows), 1
    )
    local_state = jnp.einsum("thd,the->hde", lifted_k, values, preferred_element_type=jnp.float32)
    prefix = carried_in(local_state, "ctx", add_states, jnp.zeros_like(local_state), False)
    scores = jnp.einsum("thd,shd->hts", lifted_q, lifted_k, preferred_element_type=jnp.float32)
    weights = jnp.where(causal[None], scores, 0.0).astype(jnp.bfloat16)
    prefix_low = prefix.astype(jnp.bfloat16)
    attended = jnp.einsum("hts,shd->thd", weights, values, preferred_element_type=jnp.float32)
    attended = attended + jnp.einsum(
        "thd,hde->the", lifted_q, prefix_low, preferred_element_type=jnp.float32
    )
    attended = attended.reshape(rows, width)
    sig = jax.nn.sigmoid(gate_rows.astype(jnp.float32))
    grad_out = cotangent.astype(jnp.float32)
    gated = grad_out * sig
    sumsq = lax.psum(jnp.sum(attended * attended, axis=1), "head")
    rms = jnp.sqrt(sumsq / full_width + EPSILON)[:, None]
    normed = attended / rms
    inner = lax.psum(jnp.sum(gated * normed, axis=1), "head")[:, None]
    grad_gates = (grad_out * normed * sig * (1.0 - sig)).astype(jnp.bfloat16)
    d_attn = (
        ((gated - normed * inner / full_width) / rms).astype(jnp.bfloat16).reshape(rows, heads, DH)
    )
    grad_local = jnp.einsum("thd,the->hde", lifted_q, d_attn, preferred_element_type=jnp.float32)
    suffix = carried_in(grad_local, "ctx", add_states, jnp.zeros_like(grad_local), True)
    suffix_low = suffix.astype(jnp.bfloat16)
    d_scores = jnp.einsum("the,she->hts", d_attn, values, preferred_element_type=jnp.float32)
    d_weights = jnp.where(causal[None], d_scores, 0.0).astype(jnp.bfloat16)
    grad_lq = jnp.einsum("hts,shd->thd", d_weights, lifted_k, preferred_element_type=jnp.float32)
    grad_lq = grad_lq + jnp.einsum(
        "the,hde->thd", d_attn, prefix_low, preferred_element_type=jnp.float32
    )
    grad_lk = jnp.einsum("hts,thd->shd", d_weights, lifted_q, preferred_element_type=jnp.float32)
    grad_lk = grad_lk + jnp.einsum(
        "she,hde->shd", values, suffix_low, preferred_element_type=jnp.float32
    )
    grad_v = jnp.einsum("hts,the->she", weights, d_attn, preferred_element_type=jnp.float32)
    grad_v = grad_v + jnp.einsum(
        "shd,hde->she", lifted_k, suffix_low, preferred_element_type=jnp.float32
    )
    grad_queries = (grad_lq.reshape(rows, width) * silu_slope(q_float)).astype(jnp.bfloat16)
    grad_keys = (grad_lk.reshape(rows, width) * silu_slope(k_float)).astype(jnp.bfloat16)
    grad_values = grad_v.reshape(rows, width).astype(jnp.bfloat16)
    return (grad_queries, grad_keys, grad_values, grad_gates)


def solution(mesh):
    in_specs = (
        P("ctx", "head"),
        P("ctx", "head"),
        P("ctx", "head"),
        P("ctx", "head"),
        P("ctx", "head"),
    )
    out_specs = (P("ctx", "head"), P("ctx", "head"), P("ctx", "head"), P("ctx", "head"))
    return jax.shard_map(
        per_device, mesh=mesh, in_specs=in_specs, out_specs=out_specs, check_vma=False
    )
```

profile of v0, /device:TPU:1, one launch (start us, length us, event | category | flops | bytes accessed | tf_op | source)
XLA Modules:
  0.0 394.5 jit_solution(7202193139114948521)
XLA Ops:
  7.2 1.3 fusion.26
  10.2 112.5 %all-gather.5.cloned.1.call-done = f32[256,128,128]{2,1,0:T(8,128)} async-done(((f32[4,128,128]{2,1,0:T(8,128)}), f32[256,128,128]{2,1,0:T(8,128)}) %all-gather.5.cloned.1.call-update) | async-done | bytes 16777232 | tf_op jit(solution)/shard_map/all_gather | solution.py:17
  122.7 1.0 while.22
  122.8 1.0 bitcast_add_fusion.4
  124.1 13.2 %psum.14 = f32[192]{0:T(256)S(1)} all-reduce(f32[192]{0:T(256)S(1)} %get-tuple-element.103), channel_id=1, replica_groups=mesh['ctx'=64,'head'=8] {'head'}, use_global_device_ids=true, to_apply=%region_3.4 | all-reduce | flops 192 | bytes 1536 | tf_op jit(solution)/shard_map/psum | solution.py:61
  137.3 1.3 multiply_reduce_fusion
  138.6 11.5 %psum.15 = f32[192]{0:T(256)S(1)} all-reduce(f32[192]{0:T(256)S(1)} %multiply_reduce_fusion), channel_id=1, replica_groups=mesh['ctx'=64,'head'=8] {'head'}, use_global_device_ids=true, to_apply=%region_5.6 | all-reduce | flops 192 | bytes 1536 | tf_op jit(solution)/shard_map/psum | solution.py:64
  150.0 2.0 fusion.9
  153.8 1.8 fusion.25
  156.3 165.3 %all-gather.7.cloned.1.call-done = f32[256,128,128]{2,1,0:T(8,128)} async-done(((f32[4,128,128]{2,1,0:T(8,128)}), f32[256,128,128]{2,1,0:T(8,128)}) %all-gather.7.cloned.1.call-update) | async-done | bytes 16777232 | tf_op jit(solution)/shard_map/all_gather | solution.py:17
  321.6 64.1 %while.23 = (s32[]{:T(128)}, f32[4,128,128]{2,1,0:T(8,128)S(1)}, s32[]{:T(128)}, f32[64,4,128,128]{3,2,1,0:T(8,128)}, s32[]{:T(128)}, /*index=5*/s32[]{:T(128)}, s32[]{:T(128)}, s32[]{:T(128)}) while((s32[]{:T(128)}, f32[4,128,128]{2,1,0:T(8,128)S(1)}, s32[]{:T(128)}, f32[64,4,128,128]{3,2,1,0:T(8,128)}, s32[]{:T(128)}, /*index=5*/s32[]{:T(128)}, ...), condition=%wide.region_7.8_spmd, body=%wide.region_6.7_spmd.sunk | while | flops 65542 | bytes 786575 | solution.py:24
  322.7 1.0 bitcast_add_fusion.5
  323.7 1.0 bitcast_add_fusion.5
  324.7 1.0 bitcast_add_fusion.5
  333.0 1.0 bitcast_add_fusion.5
  334.0 1.0 bitcast_add_fusion.5
  335.0 1.0 bitcast_add_fusion.5
  342.3 1.0 bitcast_add_fusion.5
  343.3 1.0 bitcast_add_fusion.5
  344.3 1.0 bitcast_add_fusion.5
  352.6 1.0 bitcast_add_fusion.5
  353.6 1.0 bitcast_add_fusion.5
  354.7 1.0 bitcast_add_fusion.5
  361.9 1.0 bitcast_add_fusion.5
  (75 shorter events, 55.9 us)
Async XLA Ops:
  7.2 1.4 copy-start
  7.2 379.6 %copy-start.1 = (bf16[192,512]{1,0:T(8,128)(2,1)S(1)}, bf16[192,512]{1,0:T(8,128)(2,1)}, u32[]{:S(2)}) copy-start(bf16[192,512]{1,0:T(8,128)(2,1)} %param.10) | copy-start | bytes 589828
  7.2 115.5 %all-gather.5.cloned.1.call-start = ((), (), s32[]{:S(2)}) async-start(), calls=%async_computation | async-start | bytes 17039360 | tf_op jit(solution)/shard_map/all_gather | solution.py:17
  9.6 312.0 %all-gather.7.cloned.1.call-start = ((), (), s32[]{:S(2)}) async-start(), calls=%async_computation.1 | async-start | bytes 17039360 | tf_op jit(solution)/shard_map/all_gather | solution.py:17
Sparse Core Ops, SparseCore 0:
  11.4 111.3 all-gather.4
  153.1 168.3 all-gather.6
where the time goes:
time: 397 us; the launch traced here: 394 us
  waiting for transfers between devices  278 us (70%)
  other arithmetic  70.8 us (18%)
  blocking collectives  24.7 us (6%)
  between operations  14.2 us (4%)
  matrix products  4.67 us (1%)
    all_gather x2, waiting for transfers between devices, carried_in(): gathered = lax.all_gather(part, axis)  278 us
    add x63, other arithmetic, add_states(): return earlier + later  63.7 us
    psum x1, blocking collectives, per_device(): sumsq = lax.psum(jnp.sum(attended * attended, axis=1), 'head')  13.2 us
    psum x1, blocking collectives, per_device(): inner = lax.psum(jnp.sum(gated * normed, axis=1), 'head')[:, None]  11.5 us
  transfers between devices with their start and end apart: 2, of which 2 were waited for; matrix products, arithmetic and copies ran while one was open for 1% of the time, Pallas kernels for 0%

commit v1 on v0

v1 whole, which is shorter than its diff:
```python
import functools

import jax
import jax.numpy as jnp
from jax import lax
from jax.experimental import pallas as pl
from jax.experimental.pallas import tpu as pltpu
from jax.sharding import PartitionSpec as P

H = 32
DH = 128
EPSILON = 1e-06
NZ = 8
F32 = jnp.float32
BF16 = jnp.bfloat16

NN = (((1,), (0,)), ((), ()))
NT = (((1,), (1,)), ((), ()))
TN = (((0,), (0,)), ((), ()))


def mm(a, b, dims):
    return lax.dot_general(a, b, dims, preferred_element_type=F32)


def silu_slope(x):
    sig = jax.nn.sigmoid(x)
    return sig * (1.0 + x * (1.0 - sig))


def kernel(
    nx, nz, nh,
    q_hbm, k_hbm, v_hbm, g_hbm, c_hbm,
    oq, ok, ov, og,
    q_ref, k_ref, v_ref, g_ref, c_ref,
    lq_ref, lk_ref, da_ref, wt_ref,
    att, gated, gg, glk, gv,
    st1, st2,
    loc, x_in, comb, a_in, p_out, e_in, f_out, f_in,
    y_out, y_in,
    in_sem, out_sem, send_sem, recv_sem, ysem,
    oq_ref, ok_ref, ov_ref, og_ref,
):
    rows, width = q_ref.shape
    heads = width // DH
    chips = nx * nz
    half = heads * DH // 2
    piece = half // chips
    me = lax.axis_index("ctx")
    hd = lax.axis_index("head")
    core = lax.rem(me, 2)
    chip = lax.div(me, 2)
    cx = lax.div(chip, nz)
    cz = lax.rem(chip, nz)
    partner = chip * 2 + (1 - core)

    ins = [
        pltpu.make_async_copy(src, dst, in_sem.at[i])
        for i, (src, dst) in enumerate(
            ((k_hbm, k_ref), (v_hbm, v_ref), (q_hbm, q_ref), (g_hbm, g_ref), (c_hbm, c_ref))
        )
    ]
    for copy in ins:
        copy.start()

    def far(i, n):
        odd = lax.rem(i, 2)
        return n // 2 + lax.div(i + 1, 2) * (1 - 2 * odd)

    def other_chip(step):
        dz = far(lax.div(step, nx), nz)
        dx = far(lax.rem(step, nx), nx)
        return lax.rem(cx + dx, nx) * nz + lax.rem(cz + dz, nz)

    barrier = pltpu.get_barrier_semaphore()

    def greet(step, carry):
        pl.semaphore_signal(barrier, inc=1, device_id={"ctx": other_chip(step) * 2 + core})
        return carry

    lax.fori_loop(0, chips - 1, greet, 0)

    def greet_head(step, carry):
        pl.semaphore_signal(barrier, inc=1, device_id={"head": lax.rem(hd + step, nh)})
        return carry

    lax.fori_loop(1, nh, greet_head, 0)
    pl.semaphore_signal(barrier, inc=1, device_id={"ctx": partner})

    def hs(h):
        return slice(h * DH, (h + 1) * DH)

    def remote(src, dst, scan, stage, device):
        return pltpu.make_async_remote_copy(
            src_ref=src,
            dst_ref=dst,
            send_sem=send_sem.at[scan, stage],
            recv_sem=recv_sem.at[scan, stage],
            device_id=device,
        )

    def scatter(src, dst, scan, stage):
        def one(step, carry):
            to = other_chip(step)
            remote(src.at[to], dst.at[chip], scan, stage, {"ctx": to * 2 + core}).start()
            return carry

        lax.fori_loop(0, chips - 1, one, 0)

    def scattered(src, dst, scan, stage):
        n = pl.ds(0, chips - 1)
        return remote(src.at[n], dst.at[n], scan, stage, {"ctx": partner})

    my_half = pl.ds(pl.multiple_of(core * half, half), half)
    other_half = pl.ds(pl.multiple_of((1 - core) * half, half), half)

    def scan_pair(scan):
        copy = remote(loc.at[scan, other_half], x_in.at[scan], scan, 0, {"ctx": partner})
        copy.start()
        return copy

    def scan_out(scan, pair):
        pair.wait_recv()
        both = loc[scan, my_half] + x_in[scan]
        comb[scan] = both.reshape(chips, piece, DH)
        scatter(comb.at[scan], a_in.at[scan], scan, 1)
        a_in[scan, chip] = comb[scan, chip]
        return scattered(comb.at[scan], a_in.at[scan], scan, 1)

    def scan_back(scan, first, reverse):
        first.wait_recv()
        total = jnp.zeros((piece, DH), F32)
        for i in range(chips):
            j = chips - 1 - i if reverse else i
            p_out[scan, j] = total
            total = total + a_in[scan, j]
        scatter(p_out.at[scan], e_in.at[scan], scan, 2)
        e_in[scan, chip] = p_out[scan, chip]
        return scattered(p_out.at[scan], e_in.at[scan], scan, 2)

    def scan_end(scan, second, reverse, state):
        second.wait_recv()
        later = 0 if reverse else 1
        mine = e_in[scan].reshape(half, DH)
        f_out[scan] = mine + jnp.where(core == later, 0.0, loc[scan, my_half])
        last = remote(f_out.at[scan], f_in.at[scan], scan, 3, {"ctx": partner})
        last.start()
        state[my_half] = (mine + jnp.where(core == later, x_in[scan], 0.0)).astype(BF16)
        last.wait_recv()
        state[other_half] = f_in[scan].astype(BF16)
        return last

    ins[0].wait()
    kf = k_ref[...].astype(F32)
    lk_ref[...] = jax.nn.silu(kf).astype(BF16)
    ins[1].wait()
    for h in range(heads):
        loc[0, hs(h)] = mm(lk_ref[:, hs(h)], v_ref[:, hs(h)], TN)
    pl.semaphore_wait(barrier, chips - 1 + 1 + nh - 1)
    pair1 = scan_pair(0)
    y_out[...] = jnp.zeros_like(y_out)
    first1 = scan_out(0, pair1)

    row = lax.broadcasted_iota(jnp.int32, (rows, rows), 0)
    col = lax.broadcasted_iota(jnp.int32, (rows, rows), 1)
    ins[2].wait()
    qf = q_ref[...].astype(F32)
    lq_ref[...] = jax.nn.silu(qf).astype(BF16)
    for h in range(heads):
        lq, lk, v = lq_ref[:, hs(h)], lk_ref[:, hs(h)], v_ref[:, hs(h)]
        w = jnp.where(row >= col, mm(lq, lk, NT), 0.0).astype(BF16)
        att[:, hs(h)] = mm(w, v, NN)
    second1 = scan_back(0, first1, False)
    ins[3].wait()
    ins[4].wait()
    sig = jax.nn.sigmoid(g_ref[...].astype(F32))
    gat = c_ref[...].astype(F32) * sig
    gated[...] = gat
    gg[...] = gat * (1.0 - sig)
    for h in range(heads):
        lq, lk = lq_ref[:, hs(h)], lk_ref[:, hs(h)]
        wt_ref[h] = jnp.where(col >= row, mm(lk, lq, NT), 0.0).astype(BF16)
    last1 = scan_end(0, second1, False, st1)

    sq = jnp.zeros((rows, DH), F32)
    dt = jnp.zeros((rows, DH), F32)
    for h in range(heads):
        a = att[:, hs(h)] + mm(lq_ref[:, hs(h)], st1[hs(h)], NN)
        att[:, hs(h)] = a
        sq = sq + a * a
        dt = dt + gated[:, hs(h)] * a

    def to_lanes(part):
        column = jnp.sum(part, axis=1, keepdims=True)
        return jnp.sum(jnp.where(row == col, column, 0.0), axis=0, keepdims=True)

    y_out[:, 0:rows] = to_lanes(sq)
    y_out[:, 256 : 256 + rows] = to_lanes(dt)

    def y_copy(src, dst, device):
        return pltpu.make_async_remote_copy(
            src_ref=src, dst_ref=dst, send_sem=ysem.at[0], recv_sem=ysem.at[1], device_id=device
        )

    def y_send(step, carry):
        to = lax.rem(hd + lax.div(nh, 2) + step, nh)
        y_copy(y_out, y_in.at[hd], {"head": to}).start()
        return carry

    lax.fori_loop(0, nh // 2, y_send, 0)
    lax.fori_loop(nh // 2 + 1, nh, y_send, 0)
    y_in[hd] = y_out[...]
    y_all = y_copy(y_in.at[pl.ds(0, nh - 1)], y_in.at[pl.ds(0, nh - 1)], {"head": lax.rem(hd + 1, nh)})
    y_all.wait_recv()
    sums = y_in[0]
    for i in range(1, nh):
        sums = sums + y_in[i]
    full = nh * width
    rinv = 1.0 / jnp.sqrt(sums[:, 0:rows] / full + EPSILON)
    coef = (sums[:, 256 : 256 + rows] * rinv / full) * rinv * rinv

    def to_column(lanes):
        return jnp.sum(jnp.where(row == col, lanes, 0.0), axis=1, keepdims=True)

    rinv_c = to_column(rinv)
    coef_c = to_column(coef)
    for h in range(heads):
        da_ref[:, hs(h)] = (gated[:, hs(h)] * rinv_c - att[:, hs(h)] * coef_c).astype(BF16)
        loc[1, hs(h)] = mm(lq_ref[:, hs(h)], da_ref[:, hs(h)], TN)
    pair2 = scan_pair(1)
    first2 = scan_out(1, pair2)

    og_ref[...] = (gg[...] * (att[...] * rinv_c)).astype(BF16)
    slope_q = silu_slope(q_ref[...].astype(F32))
    for h in range(heads):
        da, v, lk = da_ref[:, hs(h)], v_ref[:, hs(h)], lk_ref[:, hs(h)]
        dw = jnp.where(row >= col, mm(da, v, NT), 0.0).astype(BF16)
        glq = mm(dw, lk, NN) + mm(da, st1[hs(h)], NT)
        oq_ref[:, hs(h)] = (glq * slope_q[:, hs(h)]).astype(BF16)
    outs = [
        pltpu.make_async_copy(src, dst, out_sem.at[i])
        for i, (src, dst) in enumerate(((oq_ref, oq), (ok_ref, ok), (ov_ref, ov), (og_ref, og)))
    ]
    outs[0].start()
    outs[3].start()
    second2 = scan_back(1, first2, True)
    for h in range(heads):
        da, v, lq = da_ref[:, hs(h)], v_ref[:, hs(h)], lq_ref[:, hs(h)]
        dwt = jnp.where(col >= row, mm(v, da, NT), 0.0).astype(BF16)
        glk[:, hs(h)] = mm(dwt, lq, NN)
        gv[:, hs(h)] = mm(wt_ref[h], da, NN)
    gg[...] = silu_slope(k_ref[...].astype(F32))
    last2 = scan_end(1, second2, True, st2)
    for h in range(heads):
        s = st2[hs(h)]
        lk = glk[:, hs(h)] + mm(v_ref[:, hs(h)], s, NT)
        ok_ref[:, hs(h)] = (lk * gg[:, hs(h)]).astype(BF16)
        ov_ref[:, hs(h)] = (gv[:, hs(h)] + mm(lk_ref[:, hs(h)], s, NN)).astype(BF16)
    outs[1].start()
    outs[2].start()
    for sent in (pair1, first1, second1, last1, y_all, pair2, first2, second2, last2):
        sent.wait_send()
    for copy in outs:
        copy.wait()


def per_device(nx, nz, nh, queries, key_rows, value_rows, gate_rows, cotangent):
    rows, width = queries.shape
    heads = width // DH
    chips = nx * nz
    half = heads * DH // 2
    piece = half // chips
    block = pltpu.VMEM((rows, width), BF16)
    wide = pltpu.VMEM((rows, width), F32)
    pieces = pltpu.VMEM((2, chips, piece, DH), F32)
    halves = pltpu.VMEM((2, half, DH), F32)
    out = jax.ShapeDtypeStruct((rows, width), BF16)
    return pl.pallas_call(
        functools.partial(kernel, nx, nz, nh),
        out_shape=(out,) * 4,
        in_specs=[pl.BlockSpec(memory_space=pl.ANY)] * 5,
        out_specs=[pl.BlockSpec(memory_space=pl.ANY)] * 4,
        scratch_shapes=[
            block, block, block, block, block,
            block, block, block, pltpu.VMEM((heads, rows, rows), BF16),
            wide, wide, wide, wide, wide,
            pltpu.VMEM((heads * DH, DH), BF16), pltpu.VMEM((heads * DH, DH), BF16),
            pltpu.VMEM((2, heads * DH, DH), F32), halves, pieces, pieces, pieces, pieces, halves, halves,
            pltpu.VMEM((1, 512), F32), pltpu.VMEM((nh, 1, 512), F32),
            pltpu.SemaphoreType.DMA((5,)), pltpu.SemaphoreType.DMA((4,)),
            pltpu.SemaphoreType.DMA((2, 4)), pltpu.SemaphoreType.DMA((2, 4)), pltpu.SemaphoreType.DMA((2,)),
            block, block, block, block,
        ],
        compiler_params=pltpu.CompilerParams(collective_id=0, has_side_effects=True),
        name="linear_attention",
    )(queries, key_rows, value_rows, gate_rows, cotangent)


def solution(mesh):
    nh = mesh.shape["head"]
    nz = NZ
    nx = mesh.shape["ctx"] // (2 * nz)
    spec = P("ctx", "head")
    return jax.shard_map(
        functools.partial(per_device, nx, nz, nh),
        mesh=mesh, in_specs=(spec,) * 5, out_specs=(spec,) * 4, check_vma=False,
    )
```

time: 397 us -> 58.5 us (0.15)
  waiting for transfers between devices: 278 us -> 0 us
  other arithmetic: 70.8 us -> 0 us
  Pallas kernels: 0 us -> 53.3 us
  blocking collectives: 24.7 us -> 0 us
  between operations: 14.2 us -> 0.65 us
  matrix products: 4.67 us -> 0 us
    all_gather x2 -> x0, waiting for transfers between devices: 278 us -> none  [carried_in(): gathered = lax.all_gather(part, axis)]
    add x63 -> x0, other arithmetic: 63.7 us -> none  [add_states(): return earlier + later]
    pallas_call x0 -> x1, Pallas kernels: none -> 53.3 us  [per_device(): pl.pallas_call(functools.partial(kernel, nx, nz, nh), out_shape=(out,) *...]
    psum x2 -> x0, blocking collectives: 24.7 us -> none  [the longest x1 13.2 us: per_device(): sumsq = lax.psum(jnp.sum(attended * attended, axis=1), 'head')]
    dot_general x12 -> x0, matrix products: 4.67 us -> none  [the longest x1 0.98 us: per_device(): jnp.einsum('thd,the->hde', lifted_q, d_attn, preferred_element_type=jnp.f...]
    convert_element_type x3 -> x0, other arithmetic: 4.55 us -> none  [the longest x1 1.96 us: per_device(): grad_gates = (grad_out * normed * sig * (1.0 - sig)).astype(jnp.bfloat16)]
    unnamed x4 -> x10, local copies, waits for them, and re-layouts: 0.01 us -> 4.33 us
  transfers between devices with their start and end apart: 2 -> 0, of which waited for: 2 -> 0; matrix products, arithmetic and copies ran while one was open for 1% -> 0% of each run, Pallas kernels for 0% -> 0%
where the time goes in v1:
time: 58.5 us; the launch traced here: 58.3 us
  Pallas kernels  53.3 us (91%)
  local copies, waits for them, and re-layouts  4.33 us (7%)
  between operations  0.65 us (1%)
    pallas_call x1, Pallas kernels, per_device(): pl.pallas_call(functools.partial(kernel, nx, nz, nh), out_shape=(out,) *...  53.3 us
    unnamed x10, local copies, waits for them, and re-layouts  4.33 us

profile of v1, /device:TPU:1, one launch (start us, length us, event | category | flops | bytes accessed | tf_op | source)
XLA Modules:
  0.0 58.3 jit_solution(6832800743481392857)
XLA Ops:
  0.6 53.3 %linear_attention.1 = (bf16[192,512]{1,0:T(8,128)(2,1)}, bf16[192,512]{1,0:T(8,128)(2,1)}, bf16[192,512]{1,0:T(8,128)(2,1)}, bf16[192,512]{1,0:T(8,128)(2,1)}) custom-call(bf16[192,512]{1,0:T(8,128)(2,1)} %q_hbm.1, bf16[192,512]{1,0:T(8,128)(2,1)} %k_hbm.1, bf16[192,512]{1,0:T(8,128)(2,1)} %v_hbm.1, bf16[192,512]{1,0:T(8,128)(2,1)} %g_hbm.1, ...), custom_call_target="tpu_custom_call" | custom-call | tf_op jit(solution)/shard_map/linear_attention/pallas_call | solution.py:278
  54.0 0.0 copy-start.2
  54.0 1.7 %copy.13 = bf16[192,512]{1,0:T(8,128)(2,1)} copy(bf16[192,512]{1,0:T(8,128)(2,1)} %get-tuple-element.8) | data formatting | bytes 393216
  55.6 0.0 copy-done.2
  55.6 0.0 copy-start.1
  55.7 0.7 %copy.14 = bf16[192,512]{1,0:T(8,128)(2,1)} copy(bf16[192,512]{1,0:T(8,128)(2,1)S(1)} %copy-done.2) | data formatting | bytes 393216
  56.3 0.3 copy-done.1
  56.6 0.0 copy-start
  56.6 0.7 %copy.15 = bf16[192,512]{1,0:T(8,128)(2,1)} copy(bf16[192,512]{1,0:T(8,128)(2,1)S(1)} %copy-done.1) | data formatting | bytes 393216
  57.3 0.3 copy-done
  57.6 0.7 %copy.16 = bf16[192,512]{1,0:T(8,128)(2,1)} copy(bf16[192,512]{1,0:T(8,128)(2,1)S(1)} %copy-done) | data formatting | bytes 393216
Async XLA Ops:
  54.0 1.7 %copy-start.2 = (bf16[192,512]{1,0:T(8,128)(2,1)S(1)}, bf16[192,512]{1,0:T(8,128)(2,1)}, u32[]{:S(2)}) copy-start(bf16[192,512]{1,0:T(8,128)(2,1)} %get-tuple-element.9) | copy-start | bytes 589828
  55.6 1.0 %copy-start.1 = (bf16[192,512]{1,0:T(8,128)(2,1)S(1)}, bf16[192,512]{1,0:T(8,128)(2,1)}, u32[]{:S(2)}) copy-start(bf16[192,512]{1,0:T(8,128)(2,1)} %get-tuple-element.10) | copy-start | bytes 589828
  56.6 1.0 %copy-start = (bf16[192,512]{1,0:T(8,128)(2,1)S(1)}, bf16[192,512]{1,0:T(8,128)(2,1)}, u32[]{:S(2)}) copy-start(bf16[192,512]{1,0:T(8,128)(2,1)} %get-tuple-element.11) | copy-start | bytes 589828

commit v2 on v1

--- a/solution.py
+++ b/solution.py
@@ -31,15 +31,14 @@
 def kernel(
     nx, nz, nh,
     q_hbm, k_hbm, v_hbm, g_hbm, c_hbm,
-    oq, ok, ov, og,
+    oq_ref, ok_ref, ov_ref, og_ref,
     q_ref, k_ref, v_ref, g_ref, c_ref,
     lq_ref, lk_ref, da_ref, wt_ref,
     att, gated, gg, glk, gv,
     st1, st2,
     loc, x_in, comb, a_in, p_out, e_in, f_out, f_in,
     y_out, y_in,
-    in_sem, out_sem, send_sem, recv_sem, ysem,
-    oq_ref, ok_ref, ov_ref, og_ref,
+    in_sem, send_sem, recv_sem, ysem,
 ):
     rows, width = q_ref.shape
     heads = width // DH
@@ -237,12 +236,6 @@
         dw = jnp.where(row >= col, mm(da, v, NT), 0.0).astype(BF16)
         glq = mm(dw, lk, NN) + mm(da, st1[hs(h)], NT)
         oq_ref[:, hs(h)] = (glq * slope_q[:, hs(h)]).astype(BF16)
-    outs = [
-        pltpu.make_async_copy(src, dst, out_sem.at[i])
-        for i, (src, dst) in enumerate(((oq_ref, oq), (ok_ref, ok), (ov_ref, ov), (og_ref, og)))
-    ]
-    outs[0].start()
-    outs[3].start()
     second2 = scan_back(1, first2, True)
     for h in range(heads):
         da, v, lq = da_ref[:, hs(h)], v_ref[:, hs(h)], lq_ref[:, hs(h)]
@@ -256,11 +249,18 @@
         lk = glk[:, hs(h)] + mm(v_ref[:, hs(h)], s, NT)
         ok_ref[:, hs(h)] = (lk * gg[:, hs(h)]).astype(BF16)
         ov_ref[:, hs(h)] = (gv[:, hs(h)] + mm(lk_ref[:, hs(h)], s, NN)).astype(BF16)
-    outs[1].start()
-    outs[2].start()
     for sent in (pair1, first1, second1, last1, y_all, pair2, first2, second2, last2):
         sent.wait_send()
-    for copy in outs:
+
+
+def write_out(a, b, c, d, oa, ob, oc, od, sem):
+    copies = [
+        pltpu.make_async_copy(src, dst, sem.at[i])
+        for i, (src, dst) in enumerate(((a, oa), (b, ob), (c, oc), (d, od)))
+    ]
+    for copy in copies:
+        copy.start()
+    for copy in copies:
         copy.wait()
 
 
@@ -275,11 +275,11 @@
     pieces = pltpu.VMEM((2, chips, piece, DH), F32)
     halves = pltpu.VMEM((2, half, DH), F32)
     out = jax.ShapeDtypeStruct((rows, width), BF16)
-    return pl.pallas_call(
+    outs = pl.pallas_call(
         functools.partial(kernel, nx, nz, nh),
         out_shape=(out,) * 4,
-        in_specs=[pl.BlockSpec(memory_space=pl.ANY)] * 5,
-        out_specs=[pl.BlockSpec(memory_space=pl.ANY)] * 4,
+        in_specs=[pl.BlockSpec(memory_space=pltpu.HBM)] * 5,
+        out_specs=[pl.BlockSpec(memory_space=pltpu.VMEM)] * 4,
         scratch_shapes=[
             block, block, block, block, block,
             block, block, block, pltpu.VMEM((heads, rows, rows), BF16),
@@ -287,13 +287,21 @@
             pltpu.VMEM((heads * DH, DH), BF16), pltpu.VMEM((heads * DH, DH), BF16),
             pltpu.VMEM((2, heads * DH, DH), F32), halves, pieces, pieces, pieces, pieces, halves, halves,
             pltpu.VMEM((1, 512), F32), pltpu.VMEM((nh, 1, 512), F32),
-            pltpu.SemaphoreType.DMA((5,)), pltpu.SemaphoreType.DMA((4,)),
+            pltpu.SemaphoreType.DMA((5,)),
             pltpu.SemaphoreType.DMA((2, 4)), pltpu.SemaphoreType.DMA((2, 4)), pltpu.SemaphoreType.DMA((2,)),
-            block, block, block, block,
         ],
-        compiler_params=pltpu.CompilerParams(collective_id=0, has_side_effects=True),
+        compiler_params=pltpu.CompilerParams(collective_id=0, has_side_effects=True, vmem_limit_bytes=16 << 20),
         name="linear_attention",
-    )(queries, key_rows, value_rows, gate_rows, cotangent)
+    )(*(pltpu.with_memory_space_constraint(a, pltpu.HBM) for a in (queries, key_rows, value_rows, gate_rows, cotangent)))
+    return pl.pallas_call(
+        write_out,
+        out_shape=(out,) * 4,
+        in_specs=[pl.BlockSpec(memory_space=pltpu.VMEM)] * 4,
+        out_specs=[pl.BlockSpec(memory_space=pltpu.HBM)] * 4,
+        scratch_shapes=[pltpu.SemaphoreType.DMA((4,))],
+        compiler_params=pltpu.CompilerParams(vmem_limit_bytes=4 << 20),
+        name="write_out",
+    )(*outs)
 
 
 def solution(mesh):

time: 58.5 us -> 54.3 us (0.928)
  local copies, waits for them, and re-layouts: 4.33 us -> 0 us
    unnamed x10 -> x0, local copies, waits for them, and re-layouts: 4.33 us -> none
    pallas_call x0 -> x1, Pallas kernels: none -> 0.91 us  [per_device(): pl.pallas_call(write_out, out_shape=(out,) * 4, in_specs=[pl.BlockSpec(me...]
    pallas_call x1, Pallas kernels: 53.3 us -> 52.6 us  [per_device(): pl.pallas_call(functools.partial(kernel, nx, nz, nh), out_shape=(out,) *...]
where the time goes in v2:
time: 54.3 us; the launch traced here: 54.1 us
  Pallas kernels  53.5 us (99%)
  between operations  0.64 us (1%)
    pallas_call x1, Pallas kernels, per_device(): pl.pallas_call(functools.partial(kernel, nx, nz, nh), out_shape=(out,) *...  52.6 us

profile of v2, /device:TPU:1, one launch (start us, length us, event | category | flops | bytes accessed | tf_op | source)
XLA Modules:
  0.0 54.1 jit_solution(6139131492802410850)
XLA Ops:
  0.6 52.6 %linear_attention.1 = (bf16[192,512]{1,0:T(8,128)(2,1)S(1)}, bf16[192,512]{1,0:T(8,128)(2,1)S(1)}, bf16[192,512]{1,0:T(8,128)(2,1)S(1)}, bf16[192,512]{1,0:T(8,128)(2,1)S(1)}) custom-call(bf16[192,512]{1,0:T(8,128)(2,1)} %q_hbm.1, bf16[192,512]{1,0:T(8,128)(2,1)} %k_hbm.1, bf16[192,512]{1,0:T(8,128)(2,1)} %v_hbm.1, bf16[192,512]{1,0:T(8,128)(2,1)} %g_hbm.1, ...), custom_call_target="tpu_custom_call" | custom-call | tf_op jit(solution)/shard_map/linear_attention/pallas_call | solution.py:278
  53.2 0.9 %write_out.1 = (bf16[192,512]{1,0:T(8,128)(2,1)}, bf16[192,512]{1,0:T(8,128)(2,1)}, bf16[192,512]{1,0:T(8,128)(2,1)}, bf16[192,512]{1,0:T(8,128)(2,1)}) custom-call(bf16[192,512]{1,0:T(8,128)(2,1)S(1)} %get-tuple-element.8.a, bf16[192,512]{1,0:T(8,128)(2,1)S(1)} %get-tuple-element.9.b, bf16[192,512]{1,0:T(8,128)(2,1)S(1)} %get-tuple-element.10.c, ...), custom_call_target="tpu_custom_call" | custom-call | tf_op jit(solution)/shard_map/write_out/pallas_call | solution.py:296

commit v3 on v0

v3 whole, which is shorter than its diff:
```python
import functools

import jax
import jax.numpy as jnp
from jax import lax
from jax.experimental import pallas as pl
from jax.experimental.pallas import tpu as pltpu
from jax.sharding import PartitionSpec as P

H = 32
DH = 128
EPSILON = 1e-06
NZ = 8
F32 = jnp.float32
BF16 = jnp.bfloat16

NN = (((1,), (0,)), ((), ()))
NT = (((1,), (1,)), ((), ()))
TN = (((0,), (0,)), ((), ()))


def mm(a, b, dims):
    return lax.dot_general(a, b, dims, preferred_element_type=F32)


def silu_slope(x):
    sig = jax.nn.sigmoid(x)
    return sig * (1.0 + x * (1.0 - sig))


def wrap(value, n):
    return jnp.where(value >= n, value - n, value)


def offsets(nx, nz):
    def away(d, n):
        return min(d, n - d)

    every = [(dx, dz) for dz in range(nz) for dx in range(nx) if dx or dz]
    return sorted(every, key=lambda o: (-away(o[0], nx) - away(o[1], nz), -away(o[1], nz)))


def kernel(
    nx, nz, nh,
    q_hbm, k_hbm, v_hbm, g_hbm, c_hbm,
    oq, ok, ov, og,
    q_ref, k_ref, v_ref, g_ref, c_ref,
    lq_ref, lk_ref, gat, gg,
    xo, xi, pq, pk, pv,
    att, wt, da, s1,
    loc, x_in, loc2, f_out, f_in,
    comb, a_in, p_out, e_in,
    ro, ri, mine,
    y_out, y_in,
    in_sem, send_sem, recv_sem,
):
    heads, rows, _ = q_ref.shape
    hh = heads // 2
    chips = nx * nz
    piece = hh * DH // chips
    me = lax.axis_index("ctx")
    hd = lax.axis_index("head")
    core = lax.rem(me, 2)
    chip = lax.div(me, 2)
    cx = lax.div(chip, nz)
    cz = lax.rem(chip, nz)
    partner = me + 1 - 2 * core
    own = core * hh
    other = hh - own

    def load(i, src, dst):
        copies = [
            pltpu.make_async_copy(src.at[:, pl.ds(h * DH, DH)], dst.at[h], in_sem.at[i, h])
            for h in range(heads)
        ]
        for copy in copies:
            copy.start()
        return copies

    def arrived(copies):
        for copy in copies:
            copy.wait()

    k_in, v_in = load(0, k_hbm, k_ref), load(1, v_hbm, v_ref)

    xs = [wrap(cx + d, nx) * nz for d in range(nx)]
    zs = [wrap(cz + d, nz) for d in range(nz)]
    targets = [xs[dx] + zs[dz] for dx, dz in offsets(nx, nz)]
    far_heads = sorted(range(1, nh), key=lambda d: -min(d, nh - d))
    head_targets = [wrap(hd + d, nh) for d in far_heads]

    barrier = pltpu.get_barrier_semaphore()
    for to in targets:
        pl.semaphore_signal(barrier, inc=1, device_id={"ctx": to * 2 + core})
    for to in head_targets:
        pl.semaphore_signal(barrier, inc=1, device_id={"head": to})
        pl.semaphore_signal(barrier, inc=1, device_id={"ctx": partner, "head": to})
    pl.semaphore_signal(barrier, inc=1, device_id={"ctx": partner})
    q_in, g_in, c_in = load(2, q_hbm, q_ref), load(3, g_hbm, g_ref), load(4, c_hbm, c_ref)

    def remote(src, dst, stage, device):
        return pltpu.make_async_remote_copy(
            src_ref=src,
            dst_ref=dst,
            send_sem=send_sem.at[stage],
            recv_sem=recv_sem.at[stage],
            device_id=device,
        )

    def scatter(src, dst, stage):
        for to in targets:
            remote(src.at[to], dst.at[chip], stage, {"ctx": to * 2 + core}).start()
        dst[chip] = src[chip]
        n = pl.ds(0, chips - 1)
        return remote(src.at[n], dst.at[n], stage, {"ctx": partner})

    def to_partner(src, dst, stage):
        copy = remote(src, dst, stage, {"ctx": partner})
        copy.start()
        return copy

    def scan_out(scan, total):
        comb[scan] = total.reshape(chips, piece, DH)
        return scatter(comb.at[scan], a_in.at[scan], 2 * scan)

    def scan_back(scan, first, reverse):
        first.wait_recv()
        total = jnp.zeros((piece, DH), F32)
        for i in range(chips):
            j = chips - 1 - i if reverse else i
            p_out[scan, j] = total
            total = total + a_in[scan, j]
        return scatter(p_out.at[scan], e_in.at[scan], 2 * scan + 1)

    arrived(k_in)
    arrived(v_in)

    def local(h):
        lk = jax.nn.silu(k_ref[h].astype(F32)).astype(BF16)
        lk_ref[h] = lk
        loc[h] = mm(lk, v_ref[h], TN)

    for i in range(hh):
        local(other + i)
    pl.semaphore_wait(barrier, chips - 1 + 2 * (nh - 1) + 1)
    pair = to_partner(loc.at[pl.ds(other, hh)], x_in, 4)
    for i in range(hh):
        local(own + i)
    pair.wait_recv()
    first1 = scan_out(0, loc[pl.ds(own, hh)] + x_in[...])

    arrived(q_in)
    arrived(g_in)
    arrived(c_in)

    def lift(h):
        lq_ref[h] = jax.nn.silu(q_ref[h].astype(F32)).astype(BF16)
        sig = jax.nn.sigmoid(g_ref[h].astype(F32))
        gated = c_ref[h].astype(F32) * sig
        gat[h] = gated
        gg[h] = gated * (1.0 - sig)

    for i in range(hh):
        h = other + i
        lift(h)
        xo[0, i] = lq_ref[h].astype(F32)
        xo[1, i] = lk_ref[h].astype(F32)
        xo[2, i] = v_ref[h].astype(F32)
        xo[3, i] = gat[h]
    swap = to_partner(xo, xi, 5)
    row = lax.broadcasted_iota(jnp.int32, (rows, rows), 0)
    col = lax.broadcasted_iota(jnp.int32, (rows, rows), 1)
    y_out[...] = jnp.zeros_like(y_out)

    def inner(side, i, lq, lk, v):
        w = jnp.where(row >= col, mm(lq, lk, NT), 0.0).astype(BF16)
        att[side, i] = mm(w, v, NN)
        wt[side, i] = jnp.where(col >= row, mm(lk, lq, NT), 0.0).astype(BF16)

    for i in range(hh):
        lift(own + i)
        inner(0, i, lq_ref[own + i], lk_ref[own + i], v_ref[own + i])
    second1 = scan_back(0, first1, False)
    swap.wait_recv()
    for i in range(hh):
        pq[i] = xi[0, i].astype(BF16)
        pk[i] = xi[1, i].astype(BF16)
        pv[i] = xi[2, i].astype(BF16)
        inner(1, i, pq[i], pk[i], pv[i])

    def operands(side, i):
        if side == 0:
            return lq_ref[own + i], lk_ref[own + i], v_ref[own + i]
        return pq[i], pk[i], pv[i]

    second1.wait_recv()
    state = e_in[0].reshape(hh, DH, DH)
    s1[0] = (state + jnp.where(core == 1, x_in[...], 0.0)).astype(BF16)
    s1[1] = (state + jnp.where(core == 0, loc[pl.ds(own, hh)], 0.0)).astype(BF16)
    parts = []
    for side in range(2):
        sq = jnp.zeros((rows, DH), F32)
        dt = jnp.zeros((rows, DH), F32)
        for i in range(hh):
            a = att[side, i] + mm(operands(side, i)[0], s1[side, i], NN)
            att[side, i] = a
            sq = sq + a * a
            dt = dt + (gat[own + i] if side == 0 else xi[3, i]) * a
        parts += [sq, dt]
    parts = jnp.concatenate(parts, axis=1)
    pick = lax.broadcasted_iota(jnp.int32, (8, 4 * DH), 0) == lax.div(
        lax.broadcasted_iota(jnp.int32, (8, 4 * DH), 1), DH
    )
    sums = lax.dot_general(
        jnp.where(pick, 1.0, 0.0), parts, NT, precision=lax.Precision.HIGHEST, preferred_element_type=F32
    )
    y_out[core, :, 0:rows] = sums[0:2]
    y_out[1 - core, :, 0:rows] = sums[2:4]
    slot = hd * 2 + core
    for to in head_targets:
        remote(y_out, y_in.at[slot], 6, {"head": to}).start()
        remote(y_out, y_in.at[slot], 6, {"ctx": partner, "head": to}).start()
    remote(y_out, y_in.at[slot], 6, {"ctx": partner}).start()
    y_in[slot] = y_out[...]
    n = pl.ds(0, 2 * nh - 1)
    y_all = remote(y_in.at[n], y_in.at[n], 6, {"ctx": partner})
    y_all.wait_recv()
    full = nh * heads * DH
    lanes = []
    for side in range(2):
        block = core if side == 0 else 1 - core
        tot = y_in[0, block]
        for j in range(1, 2 * nh):
            tot = tot + y_in[j, block]
        rinv = 1.0 / jnp.sqrt(tot[0:1] / full + EPSILON)
        lanes += [rinv, (tot[1:2] * rinv / full) * rinv * rinv]
    sub = lax.broadcasted_iota(jnp.int32, (8, lanes[0].shape[1]), 0)
    stacked = jnp.where(sub == 0, lanes[0], jnp.where(sub == 1, lanes[1], jnp.where(sub == 2, lanes[2], lanes[3])))
    columns = jnp.transpose(stacked)[0:rows]
    rinv_c = [columns[:, 0:1], columns[:, 2:3]]
    coef_c = [columns[:, 1:2], columns[:, 3:4]]
    for side in range(2):
        for i in range(hh):
            gated = gat[own + i] if side == 0 else xi[3, i]
            d = (gated * rinv_c[side] - att[side, i] * coef_c[side]).astype(BF16)
            da[side, i] = d
            loc2[side, i] = mm(operands(side, i)[0], d, TN)
    first2 = scan_out(1, loc2[0] + loc2[1])

    def inside(side, i):
        lq, lk, v = operands(side, i)
        d = da[side, i]
        dw = jnp.where(row >= col, mm(d, v, NT), 0.0).astype(BF16)
        dwt = jnp.where(col >= row, mm(v, d, NT), 0.0).astype(BF16)
        glq = mm(dw, lk, NN) + mm(d, s1[side, i], NT)
        return att[side, i] * rinv_c[side], glq, mm(dwt, lq, NN), mm(wt[side, i], d, NN)

    for i in range(hh):
        ro[0, i], ro[1, i], ro[2, i], ro[3, i] = inside(1, i)
    back = to_partner(ro, ri, 7)
    second2 = scan_back(1, first2, True)

    def settle(h, normed, glq):
        og[h] = (gg[h] * normed).astype(BF16)
        oq[h] = (glq * silu_slope(q_ref[h].astype(F32))).astype(BF16)
        gg[h] = silu_slope(k_ref[h].astype(F32))

    for i in range(hh):
        normed, glq, mine[0, i], mine[1, i] = inside(0, i)
        settle(own + i, normed, glq)
    back.wait_recv()
    for i in range(hh):
        settle(other + i, ri[0, i], ri[1, i])

    second2.wait_recv()
    state = e_in[1].reshape(hh, DH, DH)
    f_out[...] = state + jnp.where(core == 1, loc2[0], 0.0)
    last = to_partner(f_out, f_in, 8)

    def finish(h, s, glk, gv):
        s = s.astype(BF16)
        ok[h] = ((glk + mm(v_ref[h], s, NT)) * gg[h]).astype(BF16)
        ov[h] = (gv + mm(lk_ref[h], s, NN)).astype(BF16)

    state = state + jnp.where(core == 0, loc2[1], 0.0)
    for i in range(hh):
        finish(own + i, state[i], mine[0, i], mine[1, i])
    last.wait_recv()
    for i in range(hh):
        finish(other + i, f_in[i], ri[2, i], ri[3, i])
    for sent in (pair, first1, swap, second1, y_all, first2, back, second2, last):
        sent.wait_send()


def write_out(a, b, c, d, oa, ob, oc, od, sem):
    copies = [
        pltpu.make_async_copy(src.at[h], dst.at[:, pl.ds(h * DH, DH)], sem.at[i, h])
        for i, (src, dst) in enumerate(((a, oa), (b, ob), (c, oc), (d, od)))
        for h in range(a.shape[0])
    ]
    for copy in copies:
        copy.start()
    for copy in copies:
        copy.wait()


def per_device(nx, nz, nh, *args):
    rows, width = args[0].shape
    heads = width // DH
    hh = heads // 2
    chips = nx * nz
    piece = hh * DH // chips

    def vmem(dtype, *shape):
        return pltpu.VMEM(shape, dtype)

    low = vmem(BF16, heads, rows, DH)
    wide = vmem(F32, heads, rows, DH)
    low2 = vmem(BF16, hh, rows, DH)
    four = vmem(F32, 4, hh, rows, DH)
    half = vmem(F32, hh, DH, DH)
    pieces = vmem(F32, 2, chips, piece, DH)
    out = jax.ShapeDtypeStruct((heads, rows, DH), BF16)
    outs = pl.pallas_call(
        functools.partial(kernel, nx, nz, nh),
        out_shape=(out,) * 4,
        in_specs=[pl.BlockSpec(memory_space=pltpu.HBM)] * 5,
        out_specs=[pl.BlockSpec(memory_space=pltpu.VMEM)] * 4,
        scratch_shapes=[
            low, low, low, low, low,
            low, low, wide, wide,
            four, four, low2, low2, low2,
            vmem(F32, 2, hh, rows, DH), vmem(BF16, 2, hh, rows, rows), vmem(BF16, 2, hh, rows, DH), vmem(BF16, 2, hh, DH, DH),
            vmem(F32, heads, DH, DH), half, vmem(F32, 2, hh, DH, DH), half, half,
            pieces, pieces, pieces, pieces,
            four, four, vmem(F32, 2, hh, rows, DH),
            vmem(F32, 2, 2, 256), vmem(F32, 2 * nh, 2, 2, 256),
            pltpu.SemaphoreType.DMA((5, heads)), pltpu.SemaphoreType.DMA((9,)), pltpu.SemaphoreType.DMA((9,)),
        ],
        compiler_params=pltpu.CompilerParams(collective_id=0, has_side_effects=True, vmem_limit_bytes=32 << 20),
        name="linear_attention",
    )(*(pltpu.with_memory_space_constraint(a, pltpu.HBM) for a in args))
    flat = jax.ShapeDtypeStruct((rows, width), BF16)
    return pl.pallas_call(
        write_out,
        out_shape=(flat,) * 4,
        in_specs=[pl.BlockSpec(memory_space=pltpu.VMEM)] * 4,
        out_specs=[pl.BlockSpec(memory_space=pltpu.HBM)] * 4,
        scratch_shapes=[pltpu.SemaphoreType.DMA((4, heads))],
        compiler_params=pltpu.CompilerParams(vmem_limit_bytes=4 << 20),
        name="write_out",
    )(*outs)


def solution(mesh):
    nh = mesh.shape["head"]
    nz = NZ
    nx = mesh.shape["ctx"] // (2 * nz)
    spec = P("ctx", "head")
    return jax.shard_map(
        functools.partial(per_device, nx, nz, nh),
        mesh=mesh, in_specs=(spec,) * 5, out_specs=(spec,) * 4, check_vma=False,
    )
```

time: 397 us -> 53.2 us (0.13)
  waiting for transfers between devices: 278 us -> 0 us
  other arithmetic: 70.8 us -> 0 us
  Pallas kernels: 0 us -> 52.4 us
  blocking collectives: 24.7 us -> 0 us
  between operations: 14.2 us -> 0.64 us
  matrix products: 4.67 us -> 0 us
    all_gather x2 -> x0, waiting for transfers between devices: 278 us -> none  [carried_in(): gathered = lax.all_gather(part, axis)]
    add x63 -> x0, other arithmetic: 63.7 us -> none  [add_states(): return earlier + later]
    pallas_call x0 -> x2, Pallas kernels: none -> 52.4 us  [the longest x1 51.4 us: per_device(): pl.pallas_call(functools.partial(kernel, nx, nz, nh), out_shape=(out,) *...]
    psum x2 -> x0, blocking collectives: 24.7 us -> none  [the longest x1 13.2 us: per_device(): sumsq = lax.psum(jnp.sum(attended * attended, axis=1), 'head')]
    dot_general x12 -> x0, matrix products: 4.67 us -> none  [the longest x1 0.98 us: per_device(): jnp.einsum('thd,the->hde', lifted_q, d_attn, preferred_element_type=jnp.f...]
    convert_element_type x3 -> x0, other arithmetic: 4.55 us -> none  [the longest x1 1.96 us: per_device(): grad_gates = (grad_out * normed * sig * (1.0 - sig)).astype(jnp.bfloat16)]
  transfers between devices with their start and end apart: 2 -> 0, of which waited for: 2 -> 0; matrix products, arithmetic and copies ran while one was open for 1% -> 0% of each run, Pallas kernels for 0% -> 0%
where the time goes in v3:
time: 53.2 us; the launch traced here: 53 us
  Pallas kernels  52.4 us (98%)
  between operations  0.64 us (1%)
    pallas_call x1, Pallas kernels, per_device(): pl.pallas_call(functools.partial(kernel, nx, nz, nh), out_shape=(out,) *...  51.4 us

profile of v3, /device:TPU:1, one launch (start us, length us, event | category | flops | bytes accessed | tf_op | source)
XLA Modules:
  0.0 53.0 jit_solution(15626684718752305871)
XLA Ops:
  0.6 51.4 %linear_attention.1 = (bf16[4,192,128]{2,1,0:T(8,128)(2,1)S(1)}, bf16[4,192,128]{2,1,0:T(8,128)(2,1)S(1)}, bf16[4,192,128]{2,1,0:T(8,128)(2,1)S(1)}, bf16[4,192,128]{2,1,0:T(8,128)(2,1)S(1)}) custom-call(bf16[192,512]{1,0:T(8,128)(2,1)} %q_hbm.1, bf16[192,512]{1,0:T(8,128)(2,1)} %k_hbm.1, bf16[192,512]{1,0:T(8,128)(2,1)} %v_hbm.1, bf16[192,512]{1,0:T(8,128)(2,1)} %g_hbm.1, ...), custom_call_target="tpu_custom_call" | custom-call | tf_op jit(solution)/shard_map/linear_attention/pallas_call | solution.py:324
  52.0 1.0 %write_out.1 = (bf16[192,512]{1,0:T(8,128)(2,1)}, bf16[192,512]{1,0:T(8,128)(2,1)}, bf16[192,512]{1,0:T(8,128)(2,1)}, bf16[192,512]{1,0:T(8,128)(2,1)}) custom-call(bf16[4,192,128]{2,1,0:T(8,128)(2,1)S(1)} %get-tuple-element.8.a, bf16[4,192,128]{2,1,0:T(8,128)(2,1)S(1)} %get-tuple-element.9.b, bf16[4,192,128]{2,1,0:T(8,128)(2,1)S(1)} %get-tuple-element.10.c, ...), custom_call_target="tpu_custom_call" | custom-call | tf_op jit(solution)/shard_map/write_out/pallas_call | solution.py:344

commit v4 on v3

--- a/solution.py
+++ b/solution.py
@@ -43,14 +43,14 @@
 def kernel(
     nx, nz, nh,
     q_hbm, k_hbm, v_hbm, g_hbm, c_hbm,
-    oq, ok, ov, og,
-    q_ref, k_ref, v_ref, g_ref, c_ref,
-    lq_ref, lk_ref, gat, gg,
+    oq, og, v_ref, lk_ref, glk, gv, sk, s2,
+    q_ref, k_ref, g_ref, c_ref,
+    lq_ref, gat, gg,
     xo, xi, pq, pk, pv,
-    att, wt, da, s1,
-    loc, x_in, loc2, f_out, f_in,
-    comb, a_in, p_out, e_in,
-    ro, ri, mine,
+    att, wt, da, s1, lqt,
+    loc, x_in, loc2, f_out, f_in, l_in,
+    comb, a_in, p_out, e_in, e_far,
+    ro, ri,
     y_out, y_in,
     in_sem, send_sem, recv_sem,
 ):
@@ -81,8 +81,6 @@
         for copy in copies:
             copy.wait()
 
-    k_in, v_in = load(0, k_hbm, k_ref), load(1, v_hbm, v_ref)
-
     xs = [wrap(cx + d, nx) * nz for d in range(nx)]
     zs = [wrap(cz + d, nz) for d in range(nz)]
     targets = [xs[dx] + zs[dz] for dx, dz in offsets(nx, nz)]
@@ -96,6 +94,7 @@
         pl.semaphore_signal(barrier, inc=1, device_id={"head": to})
         pl.semaphore_signal(barrier, inc=1, device_id={"ctx": partner, "head": to})
     pl.semaphore_signal(barrier, inc=1, device_id={"ctx": partner})
+    k_in, v_in = load(0, k_hbm, k_ref), load(1, v_hbm, v_ref)
     q_in, g_in, c_in = load(2, q_hbm, q_ref), load(3, g_hbm, g_ref), load(4, c_hbm, c_ref)
 
     def remote(src, dst, stage, device):
@@ -130,7 +129,11 @@
             j = chips - 1 - i if reverse else i
             p_out[scan, j] = total
             total = total + a_in[scan, j]
-        return scatter(p_out.at[scan], e_in.at[scan], 2 * scan + 1)
+        extra = None
+        if reverse:
+            extra = remote(p_out.at[scan, 0], e_far.at[chip], 9, {"ctx": 1 - core})
+            extra.start()
+        return scatter(p_out.at[scan], e_in.at[scan], 2 * scan + 1), extra
 
     arrived(k_in)
     arrived(v_in)
@@ -170,17 +173,17 @@
     swap = to_partner(xo, xi, 5)
     row = lax.broadcasted_iota(jnp.int32, (rows, rows), 0)
     col = lax.broadcasted_iota(jnp.int32, (rows, rows), 1)
-    y_out[...] = jnp.zeros_like(y_out)
 
     def inner(side, i, lq, lk, v):
         w = jnp.where(row >= col, mm(lq, lk, NT), 0.0).astype(BF16)
         att[side, i] = mm(w, v, NN)
         wt[side, i] = jnp.where(col >= row, mm(lk, lq, NT), 0.0).astype(BF16)
+        lqt[side, i] = jnp.transpose(lq)
 
     for i in range(hh):
         lift(own + i)
         inner(0, i, lq_ref[own + i], lk_ref[own + i], v_ref[own + i])
-    second1 = scan_back(0, first1, False)
+    second1, _ = scan_back(0, first1, False)
     swap.wait_recv()
     for i in range(hh):
         pq[i] = xi[0, i].astype(BF16)
@@ -207,15 +210,13 @@
             sq = sq + a * a
             dt = dt + (gat[own + i] if side == 0 else xi[3, i]) * a
         parts += [sq, dt]
-    parts = jnp.concatenate(parts, axis=1)
-    pick = lax.broadcasted_iota(jnp.int32, (8, 4 * DH), 0) == lax.div(
-        lax.broadcasted_iota(jnp.int32, (8, 4 * DH), 1), DH
-    )
-    sums = lax.dot_general(
-        jnp.where(pick, 1.0, 0.0), parts, NT, precision=lax.Precision.HIGHEST, preferred_element_type=F32
-    )
-    y_out[core, :, 0:rows] = sums[0:2]
-    y_out[1 - core, :, 0:rows] = sums[2:4]
+    lane = lax.broadcasted_iota(jnp.int32, (rows, DH), 1)
+    spread = jnp.zeros((rows, DH), F32)
+    for at, part in enumerate(parts):
+        spread = jnp.where(lane == at, jnp.sum(part, axis=1, keepdims=True), spread)
+    sums = jnp.transpose(spread)
+    y_out[core] = jnp.concatenate([sums[0:1], sums[1:2]], axis=1)
+    y_out[1 - core] = jnp.concatenate([sums[2:3], sums[3:4]], axis=1)
     slot = hd * 2 + core
     for to in head_targets:
         remote(y_out, y_in.at[slot], 6, {"head": to}).start()
@@ -232,11 +233,11 @@
         tot = y_in[0, block]
         for j in range(1, 2 * nh):
             tot = tot + y_in[j, block]
-        rinv = 1.0 / jnp.sqrt(tot[0:1] / full + EPSILON)
-        lanes += [rinv, (tot[1:2] * rinv / full) * rinv * rinv]
+        rinv = 1.0 / jnp.sqrt(tot[:, 0:rows] / full + EPSILON)
+        lanes += [rinv, (tot[:, rows : 2 * rows] * rinv / full) * rinv * rinv]
     sub = lax.broadcasted_iota(jnp.int32, (8, lanes[0].shape[1]), 0)
     stacked = jnp.where(sub == 0, lanes[0], jnp.where(sub == 1, lanes[1], jnp.where(sub == 2, lanes[2], lanes[3])))
-    columns = jnp.transpose(stacked)[0:rows]
+    columns = jnp.transpose(stacked)
     rinv_c = [columns[:, 0:1], columns[:, 2:3]]
     coef_c = [columns[:, 1:2], columns[:, 3:4]]
     for side in range(2):
@@ -244,8 +245,12 @@
             gated = gat[own + i] if side == 0 else xi[3, i]
             d = (gated * rinv_c[side] - att[side, i] * coef_c[side]).astype(BF16)
             da[side, i] = d
-            loc2[side, i] = mm(operands(side, i)[0], d, TN)
+            loc2[side, i] = mm(lqt[side, i], d, NN)
     first2 = scan_out(1, loc2[0] + loc2[1])
+
+    @pl.when(chip == 0)
+    def _():
+        to_partner(loc2.at[0], l_in, 10)
 
     def inside(side, i):
         lq, lk, v = operands(side, i)
@@ -258,48 +263,59 @@
     for i in range(hh):
         ro[0, i], ro[1, i], ro[2, i], ro[3, i] = inside(1, i)
     back = to_partner(ro, ri, 7)
-    second2 = scan_back(1, first2, True)
+    second2, extra = scan_back(1, first2, True)
 
     def settle(h, normed, glq):
         og[h] = (gg[h] * normed).astype(BF16)
         oq[h] = (glq * silu_slope(q_ref[h].astype(F32))).astype(BF16)
-        gg[h] = silu_slope(k_ref[h].astype(F32))
-
-    for i in range(hh):
-        normed, glq, mine[0, i], mine[1, i] = inside(0, i)
+        sk[h] = silu_slope(k_ref[h].astype(F32))
+
+    for i in range(hh):
+        normed, glq, glk[own + i], gv[own + i] = inside(0, i)
         settle(own + i, normed, glq)
     back.wait_recv()
     for i in range(hh):
         settle(other + i, ri[0, i], ri[1, i])
+        glk[other + i] = ri[2, i]
+        gv[other + i] = ri[3, i]
 
     second2.wait_recv()
     state = e_in[1].reshape(hh, DH, DH)
-    f_out[...] = state + jnp.where(core == 1, loc2[0], 0.0)
-    last = to_partner(f_out, f_in, 8)
-
-    def finish(h, s, glk, gv):
-        s = s.astype(BF16)
-        ok[h] = ((glk + mm(v_ref[h], s, NT)) * gg[h]).astype(BF16)
-        ov[h] = (gv + mm(lk_ref[h], s, NN)).astype(BF16)
-
-    state = state + jnp.where(core == 0, loc2[1], 0.0)
-    for i in range(hh):
-        finish(own + i, state[i], mine[0, i], mine[1, i])
-    last.wait_recv()
-    for i in range(hh):
-        finish(other + i, f_in[i], ri[2, i], ri[3, i])
-    for sent in (pair, first1, swap, second1, y_all, first2, back, second2, last):
+    s2[pl.ds(own, hh)] = (state + jnp.where(core == 0, loc2[1], 0.0)).astype(BF16)
+
+    @pl.when(chip != 0)
+    def _():
+        f_out[...] = state + jnp.where(core == 1, loc2[0], 0.0)
+        last = to_partner(f_out, f_in, 8)
+        last.wait_recv()
+        s2[pl.ds(other, hh)] = f_in[...].astype(BF16)
+        last.wait_send()
+
+    @pl.when(chip == 0)
+    def _():
+        remote(loc2.at[0], l_in, 10, {"ctx": partner}).wait()
+        remote(e_far, e_far, 9, {"ctx": partner}).wait_recv()
+        far = e_far[...].reshape(hh, DH, DH)
+        s2[pl.ds(other, hh)] = (far + jnp.where(core == 0, l_in[...], 0.0)).astype(BF16)
+
+    for sent in (pair, first1, swap, second1, y_all, first2, back, second2, extra):
         sent.wait_send()
 
 
-def write_out(a, b, c, d, oa, ob, oc, od, sem):
-    copies = [
-        pltpu.make_async_copy(src.at[h], dst.at[:, pl.ds(h * DH, DH)], sem.at[i, h])
-        for i, (src, dst) in enumerate(((a, oa), (b, ob), (c, oc), (d, od)))
-        for h in range(a.shape[0])
-    ]
-    for copy in copies:
+def finish(oq, og, v, lk, glk, gv, sk, s2, dq, dk, dv, dg, ok, ov, sem):
+    heads = oq.shape[0]
+
+    def put(i, src, dst, h):
+        copy = pltpu.make_async_copy(src.at[h], dst.at[:, pl.ds(h * DH, DH)], sem.at[i, h])
         copy.start()
+        return copy
+
+    copies = [put(0, oq, dq, h) for h in range(heads)] + [put(1, og, dg, h) for h in range(heads)]
+    for h in range(heads):
+        ok[h] = ((glk[h] + mm(v[h], s2[h], NT)) * sk[h]).astype(BF16)
+        copies.append(put(2, ok, dk, h))
+        ov[h] = (gv[h] + mm(lk[h], s2[h], NN)).astype(BF16)
+        copies.append(put(3, ov, dv, h))
     for copy in copies:
         copy.wait()
 
@@ -320,35 +336,38 @@
     four = vmem(F32, 4, hh, rows, DH)
     half = vmem(F32, hh, DH, DH)
     pieces = vmem(F32, 2, chips, piece, DH)
-    out = jax.ShapeDtypeStruct((heads, rows, DH), BF16)
+    def shape(dtype, *dims):
+        return jax.ShapeDtypeStruct(dims, dtype)
+
+    out, out_wide = shape(BF16, heads, rows, DH), shape(F32, heads, rows, DH)
     outs = pl.pallas_call(
         functools.partial(kernel, nx, nz, nh),
-        out_shape=(out,) * 4,
+        out_shape=(out, out, out, out, out_wide, out_wide, out_wide, shape(BF16, heads, DH, DH)),
         in_specs=[pl.BlockSpec(memory_space=pltpu.HBM)] * 5,
-        out_specs=[pl.BlockSpec(memory_space=pltpu.VMEM)] * 4,
+        out_specs=[pl.BlockSpec(memory_space=pltpu.VMEM)] * 8,
         scratch_shapes=[
-            low, low, low, low, low,
-            low, low, wide, wide,
+            low, low, low, low,
+            low, wide, wide,
             four, four, low2, low2, low2,
-            vmem(F32, 2, hh, rows, DH), vmem(BF16, 2, hh, rows, rows), vmem(BF16, 2, hh, rows, DH), vmem(BF16, 2, hh, DH, DH),
-            vmem(F32, heads, DH, DH), half, vmem(F32, 2, hh, DH, DH), half, half,
-            pieces, pieces, pieces, pieces,
-            four, four, vmem(F32, 2, hh, rows, DH),
-            vmem(F32, 2, 2, 256), vmem(F32, 2 * nh, 2, 2, 256),
-            pltpu.SemaphoreType.DMA((5, heads)), pltpu.SemaphoreType.DMA((9,)), pltpu.SemaphoreType.DMA((9,)),
+            vmem(F32, 2, hh, rows, DH), vmem(BF16, 2, hh, rows, rows), vmem(BF16, 2, hh, rows, DH),
+            vmem(BF16, 2, hh, DH, DH), vmem(BF16, 2, hh, DH, rows),
+            vmem(F32, heads, DH, DH), half, vmem(F32, 2, hh, DH, DH), half, half, half,
+            pieces, pieces, pieces, pieces, vmem(F32, chips, piece, DH),
+            four, four,
+            vmem(F32, 2, 1, 2 * rows), vmem(F32, 2 * nh, 2, 1, 2 * rows),
+            pltpu.SemaphoreType.DMA((5, heads)), pltpu.SemaphoreType.DMA((11,)), pltpu.SemaphoreType.DMA((11,)),
         ],
         compiler_params=pltpu.CompilerParams(collective_id=0, has_side_effects=True, vmem_limit_bytes=32 << 20),
         name="linear_attention",
     )(*(pltpu.with_memory_space_constraint(a, pltpu.HBM) for a in args))
-    flat = jax.ShapeDtypeStruct((rows, width), BF16)
     return pl.pallas_call(
-        write_out,
-        out_shape=(flat,) * 4,
-        in_specs=[pl.BlockSpec(memory_space=pltpu.VMEM)] * 4,
+        finish,
+        out_shape=(shape(BF16, rows, width),) * 4,
+        in_specs=[pl.BlockSpec(memory_space=pltpu.VMEM)] * 8,
         out_specs=[pl.BlockSpec(memory_space=pltpu.HBM)] * 4,
-        scratch_shapes=[pltpu.SemaphoreType.DMA((4, heads))],
-        compiler_params=pltpu.CompilerParams(vmem_limit_bytes=4 << 20),
-        name="write_out",
+        scratch_shapes=[low, low, pltpu.SemaphoreType.DMA((4, heads))],
+        compiler_params=pltpu.CompilerParams(vmem_limit_bytes=8 << 20),
+        name="finish",
     )(*outs)
 
 

time: 53.2 us -> 51.5 us (0.968)
  Pallas kernels: 52.4 us -> 50.6 us
    pallas_call x2, Pallas kernels: 52.4 us -> 50.6 us  [the longest x1 49.6 us: per_device(): pl.pallas_call(functools.partial(kernel, nx, nz, nh), out_shape=(out, out...]
where the time goes in v4:
time: 51.5 us; the launch traced here: 51.3 us
  Pallas kernels  50.6 us (98%)
  between operations  0.64 us (1%)
    pallas_call x1, Pallas kernels, per_device(): pl.pallas_call(functools.partial(kernel, nx, nz, nh), out_shape=(out, out...  49.6 us
    pallas_call x1, Pallas kernels, per_device(): pl.pallas_call(finish, out_shape=(shape(BF16, rows, width),) * 4, in_spec...  1.06 us

profile of v4, /device:TPU:1, one launch (start us, length us, event | category | flops | bytes accessed | tf_op | source)
XLA Modules:
  0.0 51.3 jit_solution(9330881327908653749)
XLA Ops:
  0.6 49.6 %linear_attention.1 = (bf16[4,192,128]{2,1,0:T(8,128)(2,1)S(1)}, bf16[4,192,128]{2,1,0:T(8,128)(2,1)S(1)}, bf16[4,192,128]{2,1,0:T(8,128)(2,1)S(1)}, bf16[4,192,...) custom-call(bf16[192,512]{1,0:T(8,128)(2,1)} %q_hbm.1, ...), custom_call_target="tpu_custom_call" | custom-call | tf_op jit(solution)/shard_map/linear_attention/pallas_call | solution.py:343
  50.2 1.1 %finish.1 = (bf16[192,512]{1,0:T(8,128)(2,1)}, bf16[192,512]{1,0:T(8,128)(2,1)}, bf16[192,512]{1,0:T(8,128)(2,1)}, bf16[192,512]{1,0:T(8,128)(2,1)}) custom-call(bf16[4,192,128]{2,1,0:T(8,128)(2,1)S(1)} %get-tuple-element.12.oq, bf16[4,192,128]{2,1,0:T(8,128)(2,1)S(1)} %get-tuple-element.13.og, bf16[4,192,128]{2,1,0:T(8,128)(2,1)S(1)} %get-tuple-element.14.v, ...), custom_call_target="tpu_custom_call" | custom-call | tf_op jit(solution)/shard_map/finish/pallas_call | solution.py:363

commit v5 on v4

--- a/solution.py
+++ b/solution.py
@@ -88,13 +88,21 @@
     head_targets = [wrap(hd + d, nh) for d in far_heads]
 
     barrier = pltpu.get_barrier_semaphore()
-    for to in targets:
-        pl.semaphore_signal(barrier, inc=1, device_id={"ctx": to * 2 + core})
+
+    def greet(device):
+        pl.semaphore_signal(barrier, inc=1, device_id=device)
+
+    @pl.when(core == 0)
+    def _():
+        greet({"ctx": partner})
+
+    for to in targets[:6]:
+        greet({"ctx": to * 2})
+    k_in, v_in = load(0, k_hbm, k_ref), load(1, v_hbm, v_ref)
+    for to in targets[6:]:
+        greet({"ctx": to * 2})
     for to in head_targets:
-        pl.semaphore_signal(barrier, inc=1, device_id={"head": to})
-        pl.semaphore_signal(barrier, inc=1, device_id={"ctx": partner, "head": to})
-    pl.semaphore_signal(barrier, inc=1, device_id={"ctx": partner})
-    k_in, v_in = load(0, k_hbm, k_ref), load(1, v_hbm, v_ref)
+        greet({"ctx": chip * 2, "head": to})
     q_in, g_in, c_in = load(2, q_hbm, q_ref), load(3, g_hbm, g_ref), load(4, c_hbm, c_ref)
 
     def remote(src, dst, stage, device):
@@ -143,13 +151,35 @@
         lk_ref[h] = lk
         loc[h] = mm(lk, v_ref[h], TN)
 
+    pair = remote(loc.at[pl.ds(other, hh)], x_in, 4, {"ctx": partner})
     for i in range(hh):
         local(other + i)
-    pl.semaphore_wait(barrier, chips - 1 + 2 * (nh - 1) + 1)
-    pair = to_partner(loc.at[pl.ds(other, hh)], x_in, 4)
+
+    @pl.when(core == 1)
+    def _():
+        pl.semaphore_wait(barrier, 1)
+
+    @pl.when(core == 0)
+    def _():
+        pair.wait_recv()
+
+    pair.start()
     for i in range(hh):
         local(own + i)
-    pair.wait_recv()
+
+    @pl.when(core == 1)
+    def _():
+        pair.wait_recv()
+
+    @pl.when(core == 0)
+    def _():
+        pl.semaphore_wait(barrier, 2 * (chips - 1) + 2 * (nh - 1))
+        greet({"ctx": partner})
+
+    @pl.when(core == 1)
+    def _():
+        pl.semaphore_wait(barrier, 1)
+
     first1 = scan_out(0, loc[pl.ds(own, hh)] + x_in[...])
 
     arrived(q_in)

time: 51.5 us -> 50.7 us (0.984)
  Pallas kernels: 50.6 us -> 49.9 us
    pallas_call x1, Pallas kernels: 49.6 us -> 48.8 us  [per_device(): pl.pallas_call(functools.partial(kernel, nx, nz, nh), out_shape=(out, out...]
where the time goes in v5:
time: 50.7 us; the launch traced here: 50.5 us
  Pallas kernels  49.9 us (98%)
  between operations  0.64 us (1%)
    pallas_call x1, Pallas kernels, per_device(): pl.pallas_call(functools.partial(kernel, nx, nz, nh), out_shape=(out, out...  48.8 us
    pallas_call x1, Pallas kernels, per_device(): pl.pallas_call(finish, out_shape=(shape(BF16, rows, width),) * 4, in_spec...  1.06 us

profile of v5, /device:TPU:1, one launch (start us, length us, event | category | flops | bytes accessed | tf_op | source)
XLA Modules:
  0.0 50.5 jit_solution(4179614722701255461)
XLA Ops:
  0.6 48.8 %linear_attention.1 = (bf16[4,192,128]{2,1,0:T(8,128)(2,1)S(1)}, bf16[4,192,128]{2,1,0:T(8,128)(2,1)S(1)}, bf16[4,192,128]{2,1,0:T(8,128)(2,1)S(1)}, bf16[4,192,...) custom-call(bf16[192,512]{1,0:T(8,128)(2,1)} %q_hbm.1, ...), custom_call_target="tpu_custom_call" | custom-call | tf_op jit(solution)/shard_map/linear_attention/pallas_call | solution.py:373
  49.5 1.1 %finish.1 = (bf16[192,512]{1,0:T(8,128)(2,1)}, bf16[192,512]{1,0:T(8,128)(2,1)}, bf16[192,512]{1,0:T(8,128)(2,1)}, bf16[192,512]{1,0:T(8,128)(2,1)}) custom-call(bf16[4,192,128]{2,1,0:T(8,128)(2,1)S(1)} %get-tuple-element.12.oq, bf16[4,192,128]{2,1,0:T(8,128)(2,1)S(1)} %get-tuple-element.13.og, bf16[4,192,128]{2,1,0:T(8,128)(2,1)S(1)} %get-tuple-element.14.v, ...), custom_call_target="tpu_custom_call" | custom-call | tf_op jit(solution)/shard_map/finish/pallas_call | solution.py:393

commit v6 on v5

--- a/solution.py
+++ b/solution.py
@@ -38,6 +38,9 @@
 
     every = [(dx, dz) for dz in range(nz) for dx in range(nx) if dx or dz]
     return sorted(every, key=lambda o: (-away(o[0], nx) - away(o[1], nz), -away(o[1], nz)))
+
+
+QUICK = 2
 
 
 def kernel(
@@ -48,7 +51,7 @@
     lq_ref, gat, gg,
     xo, xi, pq, pk, pv,
     att, wt, da, s1, lqt,
-    loc, x_in, loc2, f_out, f_in, l_in,
+    loc, x_in, loc2, f_out, f_in,
     comb, a_in, p_out, e_in, e_far,
     ro, ri,
     y_out, y_in,
@@ -65,6 +68,10 @@
     cx = lax.div(chip, nz)
     cz = lax.rem(chip, nz)
     partner = me + 1 - 2 * core
+    quick_chips = [x * nz for x in range(min(QUICK, nx))]
+    quick = jnp.logical_and(cz == 0, cx < QUICK)
+    give = jnp.logical_not(jnp.logical_and(quick, core == 0))
+    take = jnp.logical_not(jnp.logical_and(quick, core == 1))
     own = core * hh
     other = hh - own
 
@@ -137,11 +144,14 @@
             j = chips - 1 - i if reverse else i
             p_out[scan, j] = total
             total = total + a_in[scan, j]
-        extra = None
         if reverse:
-            extra = remote(p_out.at[scan, 0], e_far.at[chip], 9, {"ctx": 1 - core})
-            extra.start()
-        return scatter(p_out.at[scan], e_in.at[scan], 2 * scan + 1), extra
+
+            @pl.when(core == 0)
+            def _():
+                for to in quick_chips:
+                    remote(p_out.at[scan, to], e_far.at[chip], 9, {"ctx": to * 2 + 1}).start()
+
+        return scatter(p_out.at[scan], e_in.at[scan], 2 * scan + 1)
 
     arrived(k_in)
     arrived(v_in)
@@ -213,7 +223,7 @@
     for i in range(hh):
         lift(own + i)
         inner(0, i, lq_ref[own + i], lk_ref[own + i], v_ref[own + i])
-    second1, _ = scan_back(0, first1, False)
+    second1 = scan_back(0, first1, False)
     swap.wait_recv()
     for i in range(hh):
         pq[i] = xi[0, i].astype(BF16)
@@ -263,7 +273,7 @@
         tot = y_in[0, block]
         for j in range(1, 2 * nh):
             tot = tot + y_in[j, block]
-        rinv = 1.0 / jnp.sqrt(tot[:, 0:rows] / full + EPSILON)
+        rinv = lax.rsqrt(tot[:, 0:rows] / full + EPSILON)
         lanes += [rinv, (tot[:, rows : 2 * rows] * rinv / full) * rinv * rinv]
     sub = lax.broadcasted_iota(jnp.int32, (8, lanes[0].shape[1]), 0)
     stacked = jnp.where(sub == 0, lanes[0], jnp.where(sub == 1, lanes[1], jnp.where(sub == 2, lanes[2], lanes[3])))
@@ -278,10 +288,6 @@
             loc2[side, i] = mm(lqt[side, i], d, NN)
     first2 = scan_out(1, loc2[0] + loc2[1])
 
-    @pl.when(chip == 0)
-    def _():
-        to_partner(loc2.at[0], l_in, 10)
-
     def inside(side, i):
         lq, lk, v = operands(side, i)
         d = da[side, i]
@@ -293,7 +299,7 @@
     for i in range(hh):
         ro[0, i], ro[1, i], ro[2, i], ro[3, i] = inside(1, i)
     back = to_partner(ro, ri, 7)
-    second2, extra = scan_back(1, first2, True)
+    second2 = scan_back(1, first2, True)
 
     def settle(h, normed, glq):
         og[h] = (gg[h] * normed).astype(BF16)
@@ -313,22 +319,33 @@
     state = e_in[1].reshape(hh, DH, DH)
     s2[pl.ds(own, hh)] = (state + jnp.where(core == 0, loc2[1], 0.0)).astype(BF16)
 
-    @pl.when(chip != 0)
+    last = remote(f_out, f_in, 8, {"ctx": partner})
+
+    @pl.when(give)
     def _():
         f_out[...] = state + jnp.where(core == 1, loc2[0], 0.0)
-        last = to_partner(f_out, f_in, 8)
+        last.start()
+
+    @pl.when(take)
+    def _():
         last.wait_recv()
         s2[pl.ds(other, hh)] = f_in[...].astype(BF16)
+
+    @pl.when(jnp.logical_not(take))
+    def _():
+        remote(e_far, e_far, 9, {"ctx": partner}).wait_recv()
+        s2[pl.ds(other, hh)] = e_far[...].reshape(hh, DH, DH).astype(BF16)
+
+    @pl.when(give)
+    def _():
         last.wait_send()
 
-    @pl.when(chip == 0)
-    def _():
-        remote(loc2.at[0], l_in, 10, {"ctx": partner}).wait()
-        remote(e_far, e_far, 9, {"ctx": partner}).wait_recv()
-        far = e_far[...].reshape(hh, DH, DH)
-        s2[pl.ds(other, hh)] = (far + jnp.where(core == 0, l_in[...], 0.0)).astype(BF16)
-
-    for sent in (pair, first1, swap, second1, y_all, first2, back, second2, extra):
+    @pl.when(core == 0)
+    def _():
+        n = pl.ds(0, len(quick_chips))
+        remote(p_out.at[1, n], e_far.at[n], 9, {"ctx": partner}).wait_send()
+
+    for sent in (pair, first1, swap, second1, y_all, first2, back, second2):
         sent.wait_send()
 
 
@@ -381,11 +398,11 @@
             four, four, low2, low2, low2,
             vmem(F32, 2, hh, rows, DH), vmem(BF16, 2, hh, rows, rows), vmem(BF16, 2, hh, rows, DH),
             vmem(BF16, 2, hh, DH, DH), vmem(BF16, 2, hh, DH, rows),
-            vmem(F32, heads, DH, DH), half, vmem(F32, 2, hh, DH, DH), half, half, half,
+            vmem(F32, heads, DH, DH), half, vmem(F32, 2, hh, DH, DH), half, half,
             pieces, pieces, pieces, pieces, vmem(F32, chips, piece, DH),
             four, four,
             vmem(F32, 2, 1, 2 * rows), vmem(F32, 2 * nh, 2, 1, 2 * rows),
-            pltpu.SemaphoreType.DMA((5, heads)), pltpu.SemaphoreType.DMA((11,)), pltpu.SemaphoreType.DMA((11,)),
+            pltpu.SemaphoreType.DMA((5, heads)), pltpu.SemaphoreType.DMA((10,)), pltpu.SemaphoreType.DMA((10,)),
         ],
         compiler_params=pltpu.CompilerParams(collective_id=0, has_side_effects=True, vmem_limit_bytes=32 << 20),
         name="linear_attention",

time: 50.7 us -> 50.8 us (level)
  no operation moved by 1% of the time
where the time goes in v6:
time: 50.8 us; the launch traced here: 50.6 us
  Pallas kernels  50 us (98%)
  between operations  0.64 us (1%)
    pallas_call x1, Pallas kernels, per_device(): pl.pallas_call(functools.partial(kernel, nx, nz, nh), out_shape=(out, out...  48.9 us
    pallas_call x1, Pallas kernels, per_device(): pl.pallas_call(finish, out_shape=(shape(BF16, rows, width),) * 4, in_spec...  1.06 us

profile of v6, /device:TPU:1, one launch (start us, length us, event | category | flops | bytes accessed | tf_op | source)
XLA Modules:
  0.0 50.6 jit_solution(16318740475022097626)
XLA Ops:
  0.6 48.9 %linear_attention.1 = (bf16[4,192,128]{2,1,0:T(8,128)(2,1)S(1)}, bf16[4,192,128]{2,1,0:T(8,128)(2,1)S(1)}, bf16[4,192,128]{2,1,0:T(8,128)(2,1)S(1)}, bf16[4,192,...) custom-call(bf16[192,512]{1,0:T(8,128)(2,1)} %q_hbm.1, ...), custom_call_target="tpu_custom_call" | custom-call | tf_op jit(solution)/shard_map/linear_attention/pallas_call | solution.py:390
  49.5 1.1 %finish.1 = (bf16[192,512]{1,0:T(8,128)(2,1)}, bf16[192,512]{1,0:T(8,128)(2,1)}, bf16[192,512]{1,0:T(8,128)(2,1)}, bf16[192,512]{1,0:T(8,128)(2,1)}) custom-call(bf16[4,192,128]{2,1,0:T(8,128)(2,1)S(1)} %get-tuple-element.12.oq, bf16[4,192,128]{2,1,0:T(8,128)(2,1)S(1)} %get-tuple-element.13.og, bf16[4,192,128]{2,1,0:T(8,128)(2,1)S(1)} %get-tuple-element.14.v, ...), custom_call_target="tpu_custom_call" | custom-call | tf_op jit(solution)/shard_map/finish/pallas_call | solution.py:410

commit v7 on v6

--- a/solution.py
+++ b/solution.py
@@ -218,7 +218,7 @@
         w = jnp.where(row >= col, mm(lq, lk, NT), 0.0).astype(BF16)
         att[side, i] = mm(w, v, NN)
         wt[side, i] = jnp.where(col >= row, mm(lk, lq, NT), 0.0).astype(BF16)
-        lqt[side, i] = jnp.transpose(lq)
+        lqt[i, :, side * rows : (side + 1) * rows] = jnp.transpose(lq)
 
     for i in range(hh):
         lift(own + i)
@@ -284,13 +284,15 @@
         for i in range(hh):
             gated = gat[own + i] if side == 0 else xi[3, i]
             d = (gated * rinv_c[side] - att[side, i] * coef_c[side]).astype(BF16)
-            da[side, i] = d
-            loc2[side, i] = mm(lqt[side, i], d, NN)
-    first2 = scan_out(1, loc2[0] + loc2[1])
+            da[i, side * rows : (side + 1) * rows] = d
+    first2 = scan_out(1, jnp.stack([mm(lqt[i], da[i], NN) for i in range(hh)]))
+    for i in range(hh):
+        loc2[0, i] = mm(lqt[i, :, 0:rows], da[i, 0:rows], NN)
+        loc2[1, i] = mm(lqt[i, :, rows : 2 * rows], da[i, rows : 2 * rows], NN)
 
     def inside(side, i):
         lq, lk, v = operands(side, i)
-        d = da[side, i]
+        d = da[i, side * rows : (side + 1) * rows]
         dw = jnp.where(row >= col, mm(d, v, NT), 0.0).astype(BF16)
         dwt = jnp.where(col >= row, mm(v, d, NT), 0.0).astype(BF16)
         glq = mm(dw, lk, NN) + mm(d, s1[side, i], NT)
@@ -396,8 +398,8 @@
             low, low, low, low,
             low, wide, wide,
             four, four, low2, low2, low2,
-            vmem(F32, 2, hh, rows, DH), vmem(BF16, 2, hh, rows, rows), vmem(BF16, 2, hh, rows, DH),
-            vmem(BF16, 2, hh, DH, DH), vmem(BF16, 2, hh, DH, rows),
+            vmem(F32, 2, hh, rows, DH), vmem(BF16, 2, hh, rows, rows), vmem(BF16, hh, 2 * rows, DH),
+            vmem(BF16, 2, hh, DH, DH), vmem(BF16, hh, DH, 2 * rows),
             vmem(F32, heads, DH, DH), half, vmem(F32, 2, hh, DH, DH), half, half,
             pieces, pieces, pieces, pieces, vmem(F32, chips, piece, DH),
             four, four,

time: 50.8 us -> 50.8 us (level)
  no operation moved by 1% of the time
where the time goes in v7:
time: 50.8 us; the launch traced here: 50.7 us
  Pallas kernels  50 us (98%)
  between operations  0.64 us (1%)
    pallas_call x1, Pallas kernels, per_device(): pl.pallas_call(functools.partial(kernel, nx, nz, nh), out_shape=(out, out...  49 us
    pallas_call x1, Pallas kernels, per_device(): pl.pallas_call(finish, out_shape=(shape(BF16, rows, width),) * 4, in_spec...  1.06 us

profile of v7, /device:TPU:1, one launch (start us, length us, event | category | flops | bytes accessed | tf_op | source)
XLA Modules:
  0.0 50.7 jit_solution(13921708250204434717)
XLA Ops:
  0.6 49.0 %linear_attention.1 = (bf16[4,192,128]{2,1,0:T(8,128)(2,1)S(1)}, bf16[4,192,128]{2,1,0:T(8,128)(2,1)S(1)}, bf16[4,192,128]{2,1,0:T(8,128)(2,1)S(1)}, bf16[4,192,...) custom-call(bf16[192,512]{1,0:T(8,128)(2,1)} %q_hbm.1, ...), custom_call_target="tpu_custom_call" | custom-call | tf_op jit(solution)/shard_map/linear_attention/pallas_call | solution.py:392
  49.6 1.1 %finish.1 = (bf16[192,512]{1,0:T(8,128)(2,1)}, bf16[192,512]{1,0:T(8,128)(2,1)}, bf16[192,512]{1,0:T(8,128)(2,1)}, bf16[192,512]{1,0:T(8,128)(2,1)}) custom-call(bf16[4,192,128]{2,1,0:T(8,128)(2,1)S(1)} %get-tuple-element.12.oq, bf16[4,192,128]{2,1,0:T(8,128)(2,1)S(1)} %get-tuple-element.13.og, bf16[4,192,128]{2,1,0:T(8,128)(2,1)S(1)} %get-tuple-element.14.v, ...), custom_call_target="tpu_custom_call" | custom-call | tf_op jit(solution)/shard_map/finish/pallas_call | solution.py:412

commit v8 on v6

--- a/solution.py
+++ b/solution.py
@@ -40,7 +40,7 @@
     return sorted(every, key=lambda o: (-away(o[0], nx) - away(o[1], nz), -away(o[1], nz)))
 
 
-QUICK = 2
+QUICK = 1
 
 
 def kernel(

time: 50.8 us -> 50.8 us (level)
  no operation moved by 1% of the time
where the time goes in v8:
time: 50.8 us; the launch traced here: 50.6 us
  Pallas kernels  50 us (98%)
  between operations  0.64 us (1%)
    pallas_call x1, Pallas kernels, per_device(): pl.pallas_call(functools.partial(kernel, nx, nz, nh), out_shape=(out, out...  48.9 us
    pallas_call x1, Pallas kernels, per_device(): pl.pallas_call(finish, out_shape=(shape(BF16, rows, width),) * 4, in_spec...  1.06 us

profile of v8, /device:TPU:1, one launch (start us, length us, event | category | flops | bytes accessed | tf_op | source)
XLA Modules:
  0.0 50.6 jit_solution(14859214950916617505)
XLA Ops:
  0.6 48.9 %linear_attention.1 = (bf16[4,192,128]{2,1,0:T(8,128)(2,1)S(1)}, bf16[4,192,128]{2,1,0:T(8,128)(2,1)S(1)}, bf16[4,192,128]{2,1,0:T(8,128)(2,1)S(1)}, bf16[4,192,...) custom-call(bf16[192,512]{1,0:T(8,128)(2,1)} %q_hbm.1, ...), custom_call_target="tpu_custom_call" | custom-call | tf_op jit(solution)/shard_map/linear_attention/pallas_call | solution.py:390
  49.5 1.1 %finish.1 = (bf16[192,512]{1,0:T(8,128)(2,1)}, bf16[192,512]{1,0:T(8,128)(2,1)}, bf16[192,512]{1,0:T(8,128)(2,1)}, bf16[192,512]{1,0:T(8,128)(2,1)}) custom-call(bf16[4,192,128]{2,1,0:T(8,128)(2,1)S(1)} %get-tuple-element.12.oq, bf16[4,192,128]{2,1,0:T(8,128)(2,1)S(1)} %get-tuple-element.13.og, bf16[4,192,128]{2,1,0:T(8,128)(2,1)S(1)} %get-tuple-element.14.v, ...), custom_call_target="tpu_custom_call" | custom-call | tf_op jit(solution)/shard_map/finish/pallas_call | solution.py:410
